TPU v7x, 256 devices: a whole 4x4x8 slice. The times are simulated.
256 devices in a mesh: row: 16 (over x, z_lo, core), col: 16 (over z_hi, y).
Axes of the slice: x: 4, y: 4, z: 8 (z_hi: 4, z_lo: 2; z = z_hi * 2 + z_lo), core: 2. Of those that a mesh axis runs over, the one named last changes fastest.
Arguments:
- coefs: bfloat16 [1024, 16384], P('col', 'row'), may hold values from -6 to 6
- direction: bfloat16 [1024, 16384], P('col', 'row'), may hold values from -6 to 6
- tiles: bfloat16 [16, 384, 4096], P('row', 'col'), may hold values from -0.21875 to 0.21875
- block_rows: int32 [16, 384], P('row', 'col'), may hold values from 0 to 15
- block_cols: int32 [16, 384], P('row', 'col'), may hold values from 0 to 255
- counts: int32 [16, 16], P('row', 'col'), may hold values from 3 to 24, as said below
Outputs:
- h_coefs: bfloat16 [1024, 16384], P('col', 'row')
- h_direction: bfloat16 [1024, 16384], P('col', 'row')
Inputs may be any that keep to these rules, and one draw needn't show every extreme that they name: `counts`: each value lies between 3 and 24; some device's list is full in every draw. `block_cols`: tiles of one device may repeat a place.
All inputs are finite; a program needn't handle non-finite values.
Results may differ from a plain program's by a relative error of at most 0.008.
Values may be sent and summed in bfloat16 or wider, within the bound.
No kernel may reach another device: no remote copies, remote signals or barrier semaphores. Data moves between devices by JAX's collectives and lax.ppermute only.
A program may use at most 128 MiB of HBM per device.

v0:
```python
import jax
import jax.numpy as jnp
from jax import lax
from jax.sharding import PartitionSpec as P

BLOCK = 64


def make_folder(panels, row_blocks, total, piece):
    targets = lax.iota(jnp.int32, row_blocks)
    tile_flat, tile_rows, tile_cols = piece
    amount = tile_flat.shape[0]
    tile_mats = tile_flat.reshape(amount, BLOCK, BLOCK)
    picked = jnp.take(panels, tile_cols, axis=2)
    contrib = jnp.einsum("pij,sopj->psoi", tile_mats, picked, preferred_element_type=jnp.float32)
    contrib = contrib.reshape(amount, -1)
    upper = contrib.astype(jnp.bfloat16)
    lower = (contrib - upper.astype(jnp.float32)).astype(jnp.bfloat16)
    placing = (targets[:, None] == tile_rows[None, :]).astype(jnp.bfloat16)
    total = jnp.dot(placing, upper, preferred_element_type=jnp.float32)
    return total + jnp.dot(placing, lower, preferred_element_type=jnp.float32)


def finish(total, stacked, orbitals, row_blocks):
    shaped = total.reshape(row_blocks, stacked, orbitals, BLOCK).transpose(1, 2, 0, 3)
    return shaped.reshape(stacked, orbitals, row_blocks * BLOCK).astype(jnp.bfloat16)


def local(coefs, direction, tiles, block_rows, block_cols, counts):
    slots = tiles.shape[1]
    orbitals = coefs.shape[0]
    row_blocks = coefs.shape[1] // BLOCK
    slot_ids = lax.iota(jnp.int32, slots)
    used = (slot_ids < counts[0, 0]).astype(jnp.bfloat16)
    tile_flat = tiles[0] * used[:, None]
    rows_local = block_rows[0]
    cols_global = block_cols[0]
    whole_coefs, whole_direction = (
        lax.all_gather(coefs, "row", axis=1, tiled=True),
        lax.all_gather(direction, "row", axis=1, tiled=True),
    )
    all_blocks = whole_coefs.shape[1] // BLOCK
    coef_panel = whole_coefs.reshape(1, orbitals, all_blocks, BLOCK)
    direction_panel = whole_direction.reshape(1, orbitals, all_blocks, BLOCK)
    start_one = jnp.zeros((row_blocks, orbitals * BLOCK), jnp.float32)
    first_total = make_folder(
        coef_panel,
        row_blocks,
        start_one,
        (
            lax.all_gather(tile_flat, "col", axis=0, tiled=True),
            lax.all_gather(rows_local, "col", axis=0, tiled=True),
            lax.all_gather(cols_global, "col", axis=0, tiled=True),
        ),
    )
    second_total = make_folder(
        direction_panel,
        row_blocks,
        start_one,
        (
            lax.all_gather(tile_flat, "col", axis=0, tiled=True),
            lax.all_gather(rows_local, "col", axis=0, tiled=True),
            lax.all_gather(cols_global, "col", axis=0, tiled=True),
        ),
    )
    return (
        finish(first_total, 1, orbitals, row_blocks)[0],
        finish(second_total, 1, orbitals, row_blocks)[0],
    )


def solution(mesh):
    return jax.shard_map(
        local,
        mesh=mesh,
        in_specs=(
            P("col", "row"),
            P("col", "row"),
            P("row", "col", None),
            P("row", "col"),
            P("row", "col"),
            P("row", "col"),
        ),
        out_specs=(P("col", "row"), P("col", "row")),
        check_vma=False,
    )
```

profile of v0, /device:TPU:1, one launch (start us, length us, event | category | flops | bytes accessed | tf_op | source)
XLA Modules:
  0.0 238.3 jit_solution(10009733830007817194)
XLA Ops:
  9.4 1.7 bitcast_multiply_fusion
  11.1 1.3 dynamic-slice
  14.5 18.1 %all-reduce.2 = (s32[384]{0:T(512)S(1)}, s32[384]{0:T(512)S(1)}) all-reduce(s32[384]{0:T(512)S(1)} %bitcast_dynamic-update-slice_fusion, s32[384]{0:T(512)S(1)} %bitcast_dynamic-update-slice_fusion.1), channel_id=3, replica_groups=mesh['row'=16,'col'=16] {'col'}, use_global_device_ids=true, to_apply=%add.1 | all-reduce | flops 768 | bytes 6144 | tf_op jit(solution)/shard_map/all_gather | solution.py:53
  32.6 17.7 %all-gather.10.cloned.1.call-done = bf16[64,16384]{1,0:T(8,128)(2,1)} async-done(((bf16[64,1024]{1,0:T(8,128)(2,1)}), bf16[64,16384]{1,0:T(8,128)(2,1)}) %all-gather.10.cloned.1.call-update) | async-done | bytes 2097168 | tf_op jit(solution)/shard_map/all_gather | solution.py:40
  50.3 6.5 %reshape.69 = bf16[1,64,256,64]{3,2,1,0:T(8,128)(2,1)} reshape(bf16[64,16384]{1,0:T(8,128)(2,1)} %all-gather.10.cloned.1.call-done) | data formatting | bytes 4194304 | tf_op jit(solution)/shard_map/reshape | solution.py:44
  56.8 6.8 %copy.30 = bf16[1,64,256,64]{3,1,2,0:T(8,128)(2,1)} copy(bf16[1,64,256,64]{3,2,1,0:T(8,128)(2,1)} %reshape.69) | data formatting | bytes 4194304 | tf_op jit(solution)/shard_map/reshape | solution.py:44
  63.6 24.6 %all-gather.6.cloned.1.call-done = bf16[64,16384]{1,0:T(8,128)(2,1)} async-done(((bf16[64,1024]{1,0:T(8,128)(2,1)}), bf16[64,16384]{1,0:T(8,128)(2,1)}) %all-gather.6.cloned.1.call-update) | async-done | bytes 2097168 | tf_op jit(solution)/shard_map/all_gather | solution.py:39
  88.3 6.5 %reshape.65 = bf16[1,64,256,64]{3,2,1,0:T(8,128)(2,1)} reshape(bf16[64,16384]{1,0:T(8,128)(2,1)} %all-gather.6.cloned.1.call-done) | data formatting | bytes 4194304 | tf_op jit(solution)/shard_map/reshape | solution.py:43
  94.8 6.9 %copy.31 = bf16[1,64,256,64]{3,1,2,0:T(8,128)(2,1)} copy(bf16[1,64,256,64]{3,2,1,0:T(8,128)(2,1)} %reshape.65) | data formatting | bytes 4194304 | tf_op jit(solution)/shard_map/reshape | solution.py:43
  101.7 6.4 %gather_fusion.1 = bf16[384,64,64]{2,1,0:T(8,128)(2,1)} fusion(bf16[64,256,64]{2,0,1:T(8,128)(2,1)} %bitcast.60, s32[1024]{0:T(1024)S(1)} %pad_clamp_fusion), kind=kCustom, calls=%fused_computation.1.clone | custom fusion | bytes 6292992 | tf_op jit(solution)/shard_map/jit(_take)/gather | solution.py:14
  108.1 6.2 %gather_fusion = bf16[384,64,64]{2,1,0:T(8,128)(2,1)} fusion(bf16[64,256,64]{2,0,1:T(8,128)(2,1)} %bitcast.61, s32[1024]{0:T(1024)S(1)} %pad_clamp_fusion), kind=kCustom, calls=%fused_computation.clone | custom fusion | bytes 6292992 | tf_op jit(solution)/shard_map/jit(_take)/gather | solution.py:14
  114.3 43.4 %all-gather.8.cloned.1.call-done = bf16[384,4096]{1,0:T(8,128)(2,1)} async-done(((bf16[24,4096]{1,0:T(8,128)(2,1)}), bf16[384,4096]{1,0:T(8,128)(2,1)}) %all-gather.8.cloned.1.call-update) | async-done | bytes 3145744 | tf_op jit(solution)/shard_map/all_gather | solution.py:51
  157.6 3.4 %copy.20 = bf16[384,4096]{0,1:T(8,128)(2,1)S(1)} copy(bf16[384,4096]{1,0:T(8,128)(2,1)} %all-gather.8.cloned.1.call-done) | data formatting | bytes 6291456 | tf_op jit(solution)/shard_map/all_gather | solution.py:51
  161.1 9.5 %copy.21 = bf16[384,64,64]{2,1,0:T(8,128)(2,1)} copy(bf16[384,64,64]{0,2,1:T(8,128)(2,1)S(1)} %bitcast.62) | data formatting | bytes 6291456 | tf_op jit(solution)/shard_map/reshape | solution.py:13
  170.5 12.6 %fusion.1 = f32[384,64,64]{2,1,0:T(8,128)} fusion(bf16[384,64,64]{2,1,0:T(8,128)(2,1)} %copy.21, bf16[384,64,64]{2,1,0:T(8,128)(2,1)} %gather_fusion.1, pred[384]{0:T(512)(128)(4,1)S(1)} %compare_and_fusion), kind=kOutput, calls=%fused_computation.4 | convolution fusion | flops 202899456 | bytes 12583296 | tf_op jit(solution)/shard_map/pij,sopj->psoi/dot_general | solution.py:15
  183.1 11.4 %copy.26 = f32[384,64,64]{0,2,1:T(8,128)} copy(f32[384,64,64]{2,1,0:T(8,128)} %fusion.1) | data formatting | bytes 12582912 | tf_op jit(solution)/shard_map/pij,sopj->psoi/dot_general | solution.py:15
  194.5 3.5 %fusion.6 = (bf16[384,4096]{0,1:T(8,128)(2,1)S(1)}, bf16[384,4096]{0,1:T(8,128)(2,1)S(1)}) fusion(f32[384,64,64]{0,2,1:T(8,128)} %copy.26), kind=kLoop, calls=%fused_computation.10 | loop fusion | flops 6291456 | bytes 12582912 | tf_op jit(solution)/shard_map/convert_element_type | solution.py:18
  198.0 0.9 fusion.14
  198.9 0.9 fusion.11
  201.1 12.6 %fusion.4 = f32[384,64,64]{2,1,0:T(8,128)} fusion(bf16[384,64,64]{2,1,0:T(8,128)(2,1)} %copy.21, bf16[384,64,64]{2,1,0:T(8,128)(2,1)} %gather_fusion, pred[384]{0:T(512)(128)(4,1)S(1)} %compare_and_fusion), kind=kOutput, calls=%fused_computation.7 | convolution fusion | flops 202899456 | bytes 12583296 | tf_op jit(solution)/shard_map/pij,sopj->psoi/dot_general | solution.py:15
  213.7 11.4 %copy.22 = f32[384,64,64]{0,2,1:T(8,128)} copy(f32[384,64,64]{2,1,0:T(8,128)} %fusion.4) | data formatting | bytes 12582912 | tf_op jit(solution)/shard_map/pij,sopj->psoi/dot_general | solution.py:15
  225.1 3.5 %fusion.7 = (bf16[384,4096]{0,1:T(8,128)(2,1)S(1)}, bf16[384,4096]{0,1:T(8,128)(2,1)S(1)}) fusion(f32[384,64,64]{0,2,1:T(8,128)} %copy.22), kind=kLoop, calls=%fused_computation.13 | loop fusion | flops 6291456 | bytes 12582912 | tf_op jit(solution)/shard_map/convert_element_type | solution.py:18
  228.6 0.9 fusion.15
  229.5 0.9 fusion.10
  (20 shorter events, 5.6 us)
Async XLA Ops:
  7.2 43.1 %all-gather.10.cloned.1.call-start = ((), (), s32[]{:S(2)}) async-start(), calls=%async_computation.2 | async-start | bytes 2228224 | tf_op jit(solution)/shard_map/all_gather | solution.py:40
  7.9 80.4 %all-gather.6.cloned.1.call-start = ((), (), s32[]{:S(2)}) async-start(), calls=%async_computation | async-start | bytes 2228224 | tf_op jit(solution)/shard_map/all_gather | solution.py:39
  8.6 149.0 %all-gather.8.cloned.1.call-start = ((), (), s32[]{:S(2)}) async-start(), calls=%async_computation.1 | async-start | bytes 3342336 | tf_op jit(solution)/shard_map/all_gather | solution.py:51
Sparse Core Ops, SparseCore 0:
  9.8 40.4 all-gather.9
  52.1 36.1 all-gather.5
  90.7 66.8 all-gather.7
where the time goes:
time: 239 us; the launch traced here: 238 us
  waiting for transfers between devices  87.1 us (36%)
  local copies, waits for them, and re-layouts  80.3 us (34%)
  matrix products  28.8 us (12%)
  blocking collectives  18.1 us (8%)
  between operations  15.1 us (6%)
  other arithmetic  8.74 us (4%)
    all_gather x1, waiting for transfers between devices, local(): lax.all_gather(tile_flat, 'col', axis=0, tiled=True)  43.4 us
    dot_general x2, matrix products, make_folder(): jnp.einsum('pij,sopj->psoi', tile_mats, picked, preferred_element_type=jn...  25.1 us
    all_gather x1, waiting for transfers between devices, local(): lax.all_gather(coefs, 'row', axis=1, tiled=True)  24.6 us
    dot_general x2, local copies, waits for them, and re-layouts, make_folder(): jnp.einsum('pij,sopj->psoi', tile_mats, picked, preferred_element_type=jn...  22.7 us
    all_gather x1, blocking collectives, local(): lax.all_gather(cols_global, 'col', axis=0, tiled=True)  18.1 us
    all_gather x1, waiting for transfers between devices, local(): lax.all_gather(direction, 'row', axis=1, tiled=True)  17.7 us
    reshape x2, local copies, waits for them, and re-layouts, local(): coef_panel = whole_coefs.reshape(1, orbitals, all_blocks, BLOCK)  13.4 us
    reshape x2, local copies, waits for them, and re-layouts, local(): direction_panel = whole_direction.reshape(1, orbitals, all_blocks, BLOCK)  13.3 us
  transfers between devices with their start and end apart: 3, of which 3 were waited for; matrix products, arithmetic and copies ran while one was open for 18% of the time, Pallas kernels for 0%

commit v1 on v0

--- a/solution.py
+++ b/solution.py
@@ -37,7 +37,9 @@
     cols_global = block_cols[0]
     whole_coefs, whole_direction = (
         lax.all_gather(coefs, "row", axis=1, tiled=True),
-        lax.all_gather(direction, "row", axis=1, tiled=True),
+        jnp.concatenate(
+            lax.all_to_all(jnp.stack([direction] * lax.axis_size("row")), "row", 0, 0), axis=1
+        ),
     )
     all_blocks = whole_coefs.shape[1] // BLOCK
     coef_panel = whole_coefs.reshape(1, orbitals, all_blocks, BLOCK)

time: 239 us -> 217 us (0.908)
  waiting for transfers between devices: 87.1 us -> 39.6 us
  blocking collectives: 18.1 us -> 33.6 us
  starting transfers between devices: 0.11 us -> 7.23 us
    all_gather x1, waiting for transfers between devices: 24.6 us -> 0.01 us  [local(): lax.all_gather(coefs, 'row', axis=1, tiled=True)]
    all_gather x1 -> x0, waiting for transfers between devices: 17.7 us -> none  [local(): lax.all_gather(direction, 'row', axis=1, tiled=True)]
    all_gather x1, blocking collectives: 18.1 us -> 33.6 us  [local(): lax.all_gather(cols_global, 'col', axis=0, tiled=True)]
    another operation x0 -> x3, local copies, waits for them, and re-layouts: none -> 13.3 us  [the longest x2 10.8 us: local(): direction_panel = whole_direction.reshape(1, orbitals, all_blocks, BLOCK)]
    reshape x2 -> x1, local copies, waits for them, and re-layouts: 13.3 us -> 2.78 us  [local(): jnp.concatenate(lax.all_to_all(jnp.stack([direction] * lax.axis_size('row...]
    all_to_all x0 -> x1, starting transfers between devices: none -> 7.16 us  [local(): lax.all_to_all(jnp.stack([direction] * lax.axis_size('row')), 'row', 0, 0)]
    all_gather x1, waiting for transfers between devices: 43.4 us -> 38.7 us  [local(): lax.all_gather(tile_flat, 'col', axis=0, tiled=True)]
  transfers between devices with their start and end apart: 3 -> 3, of which waited for: 3 -> 2; matrix products, arithmetic and copies ran while one was open for 18% -> 21% of each run, Pallas kernels for 0% -> 0%
where the time goes in v1:
time: 217 us; the launch traced here: 216 us
  local copies, waits for them, and re-layouts  82.3 us (38%)
  waiting for transfers between devices  39.6 us (18%)
  blocking collectives  33.6 us (15%)
  matrix products  28.8 us (13%)
  between operations  15.4 us (7%)
  other arithmetic  8.74 us (4%)
  starting transfers between devices  7.23 us (3%)
    all_gather x1, waiting for transfers between devices, local(): lax.all_gather(tile_flat, 'col', axis=0, tiled=True)  38.7 us
    all_gather x1, blocking collectives, local(): lax.all_gather(cols_global, 'col', axis=0, tiled=True)  33.6 us
    dot_general x2, matrix products, make_folder(): jnp.einsum('pij,sopj->psoi', tile_mats, picked, preferred_element_type=jn...  25.1 us
    dot_general x2, local copies, waits for them, and re-layouts, make_folder(): jnp.einsum('pij,sopj->psoi', tile_mats, picked, preferred_element_type=jn...  22.7 us
    reshape x2, local copies, waits for them, and re-layouts, local(): coef_panel = whole_coefs.reshape(1, orbitals, all_blocks, BLOCK)  13.4 us
    gather x2, local copies, waits for them, and re-layouts, make_folder(): picked = jnp.take(panels, tile_cols, axis=2)  12.4 us
    another operation x2, local copies, waits for them, and re-layouts, local(): direction_panel = whole_direction.reshape(1, orbitals, all_blocks, BLOCK)  10.8 us
    reshape x1, local copies, waits for them, and re-layouts, make_folder(): tile_mats = tile_flat.reshape(amount, BLOCK, BLOCK)  9.49 us
  transfers between devices with their start and end apart: 3, of which 2 were waited for; matrix products, arithmetic and copies ran while one was open for 21% of the time, Pallas kernels for 0%

profile of v1, /device:TPU:1, one launch (start us, length us, event | category | flops | bytes accessed | tf_op | source)
XLA Modules:
  0.0 215.7 jit_solution(16712276679226359656)
XLA Ops:
  8.6 1.7 bitcast_multiply_fusion
  10.3 2.5 %stack.2 = bf16[16,64,1024]{2,1,0:T(8,128)(2,1)} broadcast(bf16[64,1024]{1,0:T(8,128)(2,1)} %param.9), dimensions={1,2} | broadcast | bytes 2228224 | tf_op jit(solution)/shard_map/stack | solution.py:41
  12.8 7.2 %all-to-all-start = ((bf16[16,64,1024]{2,1,0:T(8,128)(2,1)}), bf16[16,64,1024]{2,1,0:T(8,128)(2,1)S(1)}, u32[]{:S(2)}, u32[]{:S(2)}) async-start(bf16[16,64,1024]{2,1,0:T(8,128)(2,1)} %stack.2), calls=%async_computation | async-start | bytes 4194304 | tf_op jit(solution)/shard_map/all_to_all | solution.py:41
  21.5 33.6 %all-reduce.2 = (s32[384]{0:T(512)S(1)}, s32[384]{0:T(512)S(1)}) all-reduce(s32[384]{0:T(512)S(1)} %bitcast_dynamic-update-slice_fusion, s32[384]{0:T(512)S(1)} %bitcast_dynamic-update-slice_fusion.1), channel_id=3, replica_groups=mesh['row'=16,'col'=16] {'col'}, use_global_device_ids=true, to_apply=%add.1 | all-reduce | flops 768 | bytes 6144 | tf_op jit(solution)/shard_map/all_gather | solution.py:55
  55.3 1.3 copy-done
  56.7 2.8 %copy.24 = bf16[64,16,1024]{2,1,0:T(8,128)(2,1)S(1)} copy(bf16[64,16,1024]{2,0,1:T(8,128)(2,1)} %bitcast.64) | data formatting | bytes 4194304 | tf_op jit(solution)/shard_map/reshape | solution.py:40
  59.4 4.0 %reshape_reshape.3 = bf16[1,64,256,64]{3,2,1,0:T(8,128)(2,1)} reshape(bf16[64,16,1024]{2,1,0:T(8,128)(2,1)S(1)} %copy.24) | data formatting | bytes 4194304 | tf_op jit(solution)/shard_map/reshape;reshape | solution.py:46
  63.4 6.8 %copy.31 = bf16[1,64,256,64]{3,1,2,0:T(8,128)(2,1)} copy(bf16[1,64,256,64]{3,2,1,0:T(8,128)(2,1)} %reshape_reshape.3) | data formatting | bytes 4194304 | tf_op jit(solution)/shard_map/reshape;reshape | solution.py:46
  70.3 6.5 %reshape.67 = bf16[1,64,256,64]{3,2,1,0:T(8,128)(2,1)} reshape(bf16[64,16384]{1,0:T(8,128)(2,1)} %all-gather.5.cloned.1.call-done) | data formatting | bytes 4194304 | tf_op jit(solution)/shard_map/reshape | solution.py:45
  76.8 6.9 %copy.32 = bf16[1,64,256,64]{3,1,2,0:T(8,128)(2,1)} copy(bf16[1,64,256,64]{3,2,1,0:T(8,128)(2,1)} %reshape.67) | data formatting | bytes 4194304 | tf_op jit(solution)/shard_map/reshape | solution.py:45
  83.7 6.3 %gather_fusion.1 = bf16[384,64,64]{2,1,0:T(8,128)(2,1)} fusion(bf16[64,256,64]{2,0,1:T(8,128)(2,1)} %bitcast.61, s32[1024]{0:T(1024)S(1)} %pad_clamp_fusion), kind=kCustom, calls=%fused_computation.1.clone | custom fusion | bytes 6292992 | tf_op jit(solution)/shard_map/jit(_take)/gather | solution.py:14
  89.9 6.1 %gather_fusion = bf16[384,64,64]{2,1,0:T(8,128)(2,1)} fusion(bf16[64,256,64]{2,0,1:T(8,128)(2,1)} %bitcast.62, s32[1024]{0:T(1024)S(1)} %pad_clamp_fusion), kind=kCustom, calls=%fused_computation.clone | custom fusion | bytes 6292992 | tf_op jit(solution)/shard_map/jit(_take)/gather | solution.py:14
  96.1 38.7 %all-gather.7.cloned.1.call-done = bf16[384,4096]{1,0:T(8,128)(2,1)} async-done(((bf16[24,4096]{1,0:T(8,128)(2,1)}), bf16[384,4096]{1,0:T(8,128)(2,1)}) %all-gather.7.cloned.1.call-update) | async-done | bytes 3145744 | tf_op jit(solution)/shard_map/all_gather | solution.py:53
  134.8 3.4 %copy.20 = bf16[384,4096]{0,1:T(8,128)(2,1)S(1)} copy(bf16[384,4096]{1,0:T(8,128)(2,1)} %all-gather.7.cloned.1.call-done) | data formatting | bytes 6291456 | tf_op jit(solution)/shard_map/all_gather | solution.py:53
  138.2 9.5 %copy.21 = bf16[384,64,64]{2,1,0:T(8,128)(2,1)} copy(bf16[384,64,64]{0,2,1:T(8,128)(2,1)S(1)} %bitcast.63) | data formatting | bytes 6291456 | tf_op jit(solution)/shard_map/reshape | solution.py:13
  147.7 12.6 %fusion.1 = f32[384,64,64]{2,1,0:T(8,128)} fusion(bf16[384,64,64]{2,1,0:T(8,128)(2,1)} %copy.21, bf16[384,64,64]{2,1,0:T(8,128)(2,1)} %gather_fusion.1, pred[384]{0:T(512)(128)(4,1)S(1)} %compare_and_fusion), kind=kOutput, calls=%fused_computation.4 | convolution fusion | flops 202899456 | bytes 12583296 | tf_op jit(solution)/shard_map/pij,sopj->psoi/dot_general | solution.py:15
  160.3 11.4 %copy.27 = f32[384,64,64]{0,2,1:T(8,128)} copy(f32[384,64,64]{2,1,0:T(8,128)} %fusion.1) | data formatting | bytes 12582912 | tf_op jit(solution)/shard_map/pij,sopj->psoi/dot_general | solution.py:15
  171.6 3.5 %fusion.6 = (bf16[384,4096]{0,1:T(8,128)(2,1)S(1)}, bf16[384,4096]{0,1:T(8,128)(2,1)S(1)}) fusion(f32[384,64,64]{0,2,1:T(8,128)} %copy.27), kind=kLoop, calls=%fused_computation.10 | loop fusion | flops 6291456 | bytes 12582912 | tf_op jit(solution)/shard_map/convert_element_type | solution.py:18
  175.1 0.9 fusion.14
  176.0 0.9 fusion.11
  178.3 12.6 %fusion.4 = f32[384,64,64]{2,1,0:T(8,128)} fusion(bf16[384,64,64]{2,1,0:T(8,128)(2,1)} %copy.21, bf16[384,64,64]{2,1,0:T(8,128)(2,1)} %gather_fusion, pred[384]{0:T(512)(128)(4,1)S(1)} %compare_and_fusion), kind=kOutput, calls=%fused_computation.7 | convolution fusion | flops 202899456 | bytes 12583296 | tf_op jit(solution)/shard_map/pij,sopj->psoi/dot_general | solution.py:15
  190.8 11.4 %copy.22 = f32[384,64,64]{0,2,1:T(8,128)} copy(f32[384,64,64]{2,1,0:T(8,128)} %fusion.4) | data formatting | bytes 12582912 | tf_op jit(solution)/shard_map/pij,sopj->psoi/dot_general | solution.py:15
  202.2 3.5 %fusion.7 = (bf16[384,4096]{0,1:T(8,128)(2,1)S(1)}, bf16[384,4096]{0,1:T(8,128)(2,1)S(1)}) fusion(f32[384,64,64]{0,2,1:T(8,128)} %copy.22), kind=kLoop, calls=%fused_computation.13 | loop fusion | flops 6291456 | bytes 12582912 | tf_op jit(solution)/shard_map/convert_element_type | solution.py:18
  206.7 0.9 fusion.10
  (29 shorter events, 5.4 us)
Async XLA Ops:
  7.2 12.8 %copy-start.3 = (u32[256]{0:T(256)S(1)}, u32[256]{0:T(256)}, u32[]{:S(2)}) copy-start(u32[256]{0:T(256)} %constant.16) | copy-start | bytes 3076
  7.2 14.1 %copy-start.1 = (s32[1,24]{1,0:T(1,128)S(1)}, s32[1,24]{1,0:T(1,128)}, u32[]{:S(2)}) copy-start(s32[1,24]{1,0:T(1,128)} %param.12) | copy-start | bytes 292
  7.2 14.2 %copy-start.2 = (s32[1,24]{1,0:T(1,128)S(1)}, s32[1,24]{1,0:T(1,128)}, u32[]{:S(2)}) copy-start(s32[1,24]{1,0:T(1,128)} %param.11) | copy-start | bytes 292
  7.2 63.1 %all-gather.5.cloned.1.call-start = ((), (), s32[]{:S(2)}) async-start(), calls=%async_computation.1 | async-start | bytes 2228224 | tf_op jit(solution)/shard_map/all_gather | solution.py:39
  7.9 126.8 %all-gather.7.cloned.1.call-start = ((), (), s32[]{:S(2)}) async-start(), calls=%async_computation.2 | async-start | bytes 3342336 | tf_op jit(solution)/shard_map/all_gather | solution.py:53
  12.8 42.5 %all-to-all-start = ((bf16[16,64,1024]{2,1,0:T(8,128)(2,1)}), bf16[16,64,1024]{2,1,0:T(8,128)(2,1)S(1)}, u32[]{:S(2)}, u32[]{:S(2)}) async-start(bf16[16,64,1024]{2,1,0:T(8,128)(2,1)} %stack.2), calls=%async_computation | async-start | bytes 4194304 | tf_op jit(solution)/shard_map/all_to_all | solution.py:41
  55.3 1.3 copy-start
Sparse Core Ops, SparseCore 0:
  9.8 54.1 all-gather.4
  66.5 68.2 all-gather.6
